TPU v7x, 256 devices: a whole 4x4x8 slice. The times are simulated.
256 devices in a mesh: dp: 16 (over y, x), mem: 16 (over z, core).
Axes of the slice: x: 4, y: 4, z: 8, core: 2. Of those that a mesh axis runs over, the one named last changes fastest.
Arguments:
- grad_out: bfloat16 [2048, 4096], P('dp', 'mem'), may hold values from -16 to 16
- values: bfloat16 [4096, 4096], P('dp', 'mem'), may hold values from -0.0234375 to 0.0234375
- slot_rows: int32 [2048, 32], P('dp'), may hold values from 0 to 4095, all different within a row
- weights: float32 [2048, 32], P('dp'), may hold values from 0 to 1, as said below
- sub_picks: int32 [2, 2048, 32], P(None, 'dp'), may hold values from 0 to 1023
- queries: bfloat16 [2048, 1024], P('dp'), may hold values from -6 to 6
- sub_keys: bfloat16 [2, 1024, 512], replicated, may hold values from -0.25 to 0.25
- layer_input: bfloat16 [2048, 4096], P('dp', 'mem'), may hold values from -6 to 6
Outputs:
- value_grad: float32 [4096, 4096], P('dp', 'mem')
- key_grad: float32 [2, 1024, 512], P(None, 'dp')
- proj_grad: float32 [1024, 4096], P('dp', 'mem')
Inputs may be any that keep to these rules, and one draw needn't show every extreme that they name: `slot_rows`: the 32 value rows of one token are distinct, and every value row is read by some token. Each token's 32 weights are positive and sum to one.
All inputs are finite; a program needn't handle non-finite values.
Results may differ from a plain program's by a relative error of at most 0.004.
Values may be sent and summed in bfloat16 or wider, within the bound.
No kernel may reach another device: no remote copies, remote signals or barrier semaphores. Data moves between devices by JAX's collectives and lax.ppermute only.
A program may use at most 64 MiB of HBM per device.

v0:
```python
import jax
import jax.numpy as jnp
from jax import lax
from jax.sharding import PartitionSpec as P

highest = lax.Precision.HIGHEST


def split_hot(offsets, blocks, block_width, table_type):
    inside_mask = (offsets >= 0) & (offsets < blocks * block_width)
    clipped = jnp.where(inside_mask, offsets, 0)
    block_ids = clipped // block_width
    within_ids = clipped - block_ids * block_width
    block_hot = (
        (block_ids[:, :, None] == jnp.arange(blocks, dtype=jnp.int32)) & inside_mask[:, :, None]
    ).astype(table_type)
    within_hot = (within_ids[:, :, None] == jnp.arange(block_width, dtype=jnp.int32)).astype(
        table_type
    )
    return (block_hot, within_hot)


def value_block(grad_rows, row_ids, row_weights, values, owner_start):
    val_rows = values.shape[0]
    blocks = val_rows // 128
    row_count = grad_rows.shape[0]
    block_hot, within_hot = split_hot(row_ids - owner_start, blocks, 128, jnp.bfloat16)
    weighted = block_hot * row_weights[:, :, None]
    bag_wide = jnp.einsum("tkb,tkc->tbc", weighted, within_hot, preferred_element_type=jnp.float32)
    bag_rows = bag_wide.reshape(row_count, val_rows).astype(jnp.bfloat16)
    value_term = lax.dot_general(
        bag_rows, grad_rows, (((0,), (0,)), ((), ())), preferred_element_type=jnp.float32
    )
    scores = lax.dot_general(
        grad_rows, values, (((1,), (1,)), ((), ())), preferred_element_type=jnp.float32
    )
    scores = scores.reshape(row_count, blocks, 128)
    picked = jnp.einsum(
        "tbc,tkb->tkc",
        scores,
        block_hot.astype(jnp.float32),
        precision=highest,
        preferred_element_type=jnp.float32,
    )
    slot_term = jnp.sum(picked * within_hot.astype(jnp.float32), axis=2)
    return (value_term, slot_term)


def body(grad_out, values, slot_rows, weights, sub_picks, queries, sub_keys, layer_input):
    val_rows = values.shape[0]
    slot_count = slot_rows.shape[1]
    groups = lax.axis_size("dp")
    owner_start = lax.axis_index("dp") * val_rows
    vweights = weights.astype(jnp.bfloat16)
    start_acc = jnp.zeros((val_rows, values.shape[1]), jnp.float32)
    value_acc = start_acc
    grad_rows = lax.all_gather(grad_out, "dp", axis=0, tiled=True)
    row_ids = lax.all_gather(slot_rows, "dp", axis=0, tiled=True)
    row_weights = lax.all_gather(vweights, "dp", axis=0, tiled=True)
    row_count = grad_rows.shape[0]
    block_rows = 512
    steps_count = row_count // block_rows

    def one_block(acc_now, blocked):
        value_term, slot_term = value_block(blocked[0], blocked[1], blocked[2], values, owner_start)
        return (acc_now + value_term, slot_term)

    stacked = (
        grad_rows.reshape(steps_count, block_rows, grad_rows.shape[1]),
        row_ids.reshape(steps_count, block_rows, slot_count),
        row_weights.reshape(steps_count, block_rows, slot_count),
    )
    value_acc, slot_terms = lax.scan(one_block, value_acc, stacked)
    slot_all = slot_terms.reshape(row_count, slot_count)
    value_grad, slot_all = (value_acc, slot_all)
    slot_grad = lax.psum(lax.psum_scatter(slot_all, "dp", scatter_dimension=0, tiled=True), "mem")
    centered = slot_grad - jnp.sum(weights * slot_grad, axis=1, keepdims=True)
    score_grad = weights * centered
    own_count = score_grad.shape[0]
    sub_count = sub_keys.shape[1]
    key_width = sub_keys.shape[2]
    sub_width = 128
    halves = []
    for half_index in range(2):
        block_hot, within_hot = split_hot(
            sub_picks[half_index], sub_count // sub_width, sub_width, jnp.float32
        )
        weighted = block_hot * score_grad[:, :, None]
        summed = jnp.einsum(
            "tkb,tkc->tbc",
            weighted,
            within_hot,
            precision=highest,
            preferred_element_type=jnp.float32,
        )
        halves.append(summed.reshape(own_count, sub_count))
    sub_grad = jnp.stack(halves, axis=1).astype(jnp.bfloat16)
    query_pairs = queries.reshape(own_count, 2, key_width)
    mem_count = lax.axis_size("mem")
    piece_rows = sub_count // (groups * mem_count)
    sub_view = sub_grad.reshape(own_count, 2, groups, mem_count, piece_rows)
    own_piece = lax.dynamic_slice_in_dim(sub_view, lax.axis_index("mem"), 1, 3)
    key_source = own_piece.reshape(own_count, 2, groups * piece_rows)
    key_part = jnp.einsum(
        "thc,the->hce", key_source, query_pairs, preferred_element_type=jnp.float32
    )
    dquery = jnp.einsum("thc,hce->the", sub_grad, sub_keys, preferred_element_type=jnp.float32)
    dquery = dquery.reshape(own_count, 2 * key_width).astype(jnp.bfloat16)
    key_grad = lax.psum_scatter(key_part, "dp", scatter_dimension=1, tiled=True)
    proj_grad = lax.psum_scatter(
        lax.dot_general(
            dquery, layer_input, (((0,), (0,)), ((), ())), preferred_element_type=jnp.float32
        ),
        "dp",
        scatter_dimension=0,
        tiled=True,
    )
    key_grad = lax.all_gather(key_grad, "mem", axis=1, tiled=True)
    return (value_grad, key_grad, proj_grad)


def solution(mesh):
    return jax.shard_map(
        body,
        mesh=mesh,
        in_specs=(
            P("dp", "mem"),
            P("dp", "mem"),
            P("dp", None),
            P("dp", None),
            P(None, "dp", None),
            P("dp", None),
            P(),
            P("dp", "mem"),
        ),
        out_specs=(P("dp", "mem"), P(None, "dp", None), P("dp", "mem")),
        check_vma=False,
    )
```

profile of v0, /device:TPU:2, one launch (start us, length us, event | category | flops | bytes accessed | tf_op | source)
XLA Modules:
  0.0 467.8 jit_solution(13477727605715217793)
XLA Ops:
  8.0 25.9 %all_gather.12 = s32[2048,32]{0,1:T(8,128)} all-gather(s32[128,32]{0,1:T(8,128)} %param.12), channel_id=1, replica_groups=mesh['dp'=16,'mem'=16] {'dp'}, dimensions={0}, use_global_device_ids=true | all-gather | bytes 278528 | tf_op jit(solution)/shard_map/all_gather | solution.py:58
  33.8 1.3 copy.38
  35.9 22.0 %all_gather.13 = bf16[2048,32]{0,1:T(8,128)(2,1)S(1)} all-gather(bf16[128,32]{0,1:T(8,128)(2,1)S(1)} %convert_element_type.41), channel_id=1, replica_groups=mesh['dp'=16,'mem'=16] {'dp'}, dimensions={0}, use_global_device_ids=true | all-gather | bytes 139264 | tf_op jit(solution)/shard_map/all_gather | solution.py:59
  57.8 1.0 copy.39
  58.9 1.7 all-gather.2.cloned.1.call-done
  60.5 90.1 %while.15 = (s32[]{:T(128)}, f32[256,256]{1,0:T(8,128)S(1)}, f32[4,512,32]{2,1,0:T(8,128)}, s32[4,512,32]{2,1,0:T(8,128)S(1)}, s32[]{:T(128)}, /*index=5*/bf16[4...) while((s32[]{:T(128)}, f32[256,256]{1,0:T(8,128)S(1)}, ...), condition=%wide.region_2.3_spmd.clone, body=%wide.region_0.2_spmd.clone.sunk | while | flops 206569472 | bytes 4358351 | solution.py:73
  62.0 4.8 %fusion.85 = bf16[512,2,128]{2,1,0:T(2,128)(2,1)} fusion(s32[512,32]{1,0:T(8,128)S(1)} %multiply_subtract_fusion.4, pred[512,32]{1,0:T(8,128)(4,1)S(1)} %get-tuple-element.212, s32[512,32]{1,0:T(8,128)S(1)} %get-tuple-element.213, bf16[512,32]{1,0:T(8,128)(2,1)S(1)} %dynamic-slice_bitcast_fusion.2), kind=kOutput, calls=%fused_computation.5.clone.1 | convolution fusion | flops 10715136 | bytes 442368 | tf_op jit(solution)/shard_map/while/body/eval_jaxpr/tkb,tkc->tbc/dot_general | solution.py:29
  66.8 1.3 convolution_add_fusion.2
  68.1 1.2 fusion.86
  69.4 13.0 %multiply_reduce_fusion.3 = f32[512,32]{1,0:T(8,128)S(1)} fusion(s32[512,32]{1,0:T(8,128)} %copy-done.3, f32[512,2,128]{2,0,1:T(8,128)S(1)} %fusion.86, pred[512,32]{1,0:T(8,128)(4,1)S(1)} %get-tuple-element.212, s32[512,32]{1,0:T(8,128)} %copy-done.2), kind=kOutput, calls=%fused_computation.clone.1 | convolution fusion | flops 60866560 | bytes 737280 | tf_op jit(solution)/shard_map/while/body/eval_jaxpr/tbc,tkb->tkc/dot_general | solution.py:38
  84.5 4.8 %fusion.85 = bf16[512,2,128]{2,1,0:T(2,128)(2,1)} fusion(s32[512,32]{1,0:T(8,128)S(1)} %multiply_subtract_fusion.4, pred[512,32]{1,0:T(8,128)(4,1)S(1)} %get-tuple-element.212, s32[512,32]{1,0:T(8,128)S(1)} %get-tuple-element.213, bf16[512,32]{1,0:T(8,128)(2,1)S(1)} %dynamic-slice_bitcast_fusion.2), kind=kOutput, calls=%fused_computation.5.clone.1 | convolution fusion | flops 10715136 | bytes 442368 | tf_op jit(solution)/shard_map/while/body/eval_jaxpr/tkb,tkc->tbc/dot_general | solution.py:29
  89.3 1.3 convolution_add_fusion.2
  90.6 1.2 fusion.86
  91.9 13.0 %multiply_reduce_fusion.3 = f32[512,32]{1,0:T(8,128)S(1)} fusion(s32[512,32]{1,0:T(8,128)} %copy-done.3, f32[512,2,128]{2,0,1:T(8,128)S(1)} %fusion.86, pred[512,32]{1,0:T(8,128)(4,1)S(1)} %get-tuple-element.212, s32[512,32]{1,0:T(8,128)} %copy-done.2), kind=kOutput, calls=%fused_computation.clone.1 | convolution fusion | flops 60866560 | bytes 737280 | tf_op jit(solution)/shard_map/while/body/eval_jaxpr/tbc,tkb->tkc/dot_general | solution.py:38
  107.0 4.8 %fusion.85 = bf16[512,2,128]{2,1,0:T(2,128)(2,1)} fusion(s32[512,32]{1,0:T(8,128)S(1)} %multiply_subtract_fusion.4, pred[512,32]{1,0:T(8,128)(4,1)S(1)} %get-tuple-element.212, s32[512,32]{1,0:T(8,128)S(1)} %get-tuple-element.213, bf16[512,32]{1,0:T(8,128)(2,1)S(1)} %dynamic-slice_bitcast_fusion.2), kind=kOutput, calls=%fused_computation.5.clone.1 | convolution fusion | flops 10715136 | bytes 442368 | tf_op jit(solution)/shard_map/while/body/eval_jaxpr/tkb,tkc->tbc/dot_general | solution.py:29
  111.8 1.3 convolution_add_fusion.2
  113.2 1.2 fusion.86
  114.4 13.0 %multiply_reduce_fusion.3 = f32[512,32]{1,0:T(8,128)S(1)} fusion(s32[512,32]{1,0:T(8,128)} %copy-done.3, f32[512,2,128]{2,0,1:T(8,128)S(1)} %fusion.86, pred[512,32]{1,0:T(8,128)(4,1)S(1)} %get-tuple-element.212, s32[512,32]{1,0:T(8,128)} %copy-done.2), kind=kOutput, calls=%fused_computation.clone.1 | convolution fusion | flops 60866560 | bytes 737280 | tf_op jit(solution)/shard_map/while/body/eval_jaxpr/tbc,tkb->tkc/dot_general | solution.py:38
  129.5 4.8 %fusion.85 = bf16[512,2,128]{2,1,0:T(2,128)(2,1)} fusion(s32[512,32]{1,0:T(8,128)S(1)} %multiply_subtract_fusion.4, pred[512,32]{1,0:T(8,128)(4,1)S(1)} %get-tuple-element.212, s32[512,32]{1,0:T(8,128)S(1)} %get-tuple-element.213, bf16[512,32]{1,0:T(8,128)(2,1)S(1)} %dynamic-slice_bitcast_fusion.2), kind=kOutput, calls=%fused_computation.5.clone.1 | convolution fusion | flops 10715136 | bytes 442368 | tf_op jit(solution)/shard_map/while/body/eval_jaxpr/tkb,tkc->tbc/dot_general | solution.py:29
  134.3 1.3 convolution_add_fusion.2
  135.7 1.2 fusion.86
  136.9 13.0 %multiply_reduce_fusion.3 = f32[512,32]{1,0:T(8,128)S(1)} fusion(s32[512,32]{1,0:T(8,128)} %copy-done.3, f32[512,2,128]{2,0,1:T(8,128)S(1)} %fusion.86, pred[512,32]{1,0:T(8,128)(4,1)S(1)} %get-tuple-element.212, s32[512,32]{1,0:T(8,128)} %copy-done.2), kind=kOutput, calls=%fused_computation.clone.1 | convolution fusion | flops 60866560 | bytes 737280 | tf_op jit(solution)/shard_map/while/body/eval_jaxpr/tbc,tkb->tkc/dot_general | solution.py:38
  150.6 2.3 copy.42
  153.8 77.3 %reduce-scatter.4.cloned.1.call-done = f32[128,32]{0,1:T(8,128)} async-done(((f32[2048,32]{0,1:T(8,128)}), f32[128,32]{0,1:T(8,128)}) %reduce-scatter.4.cloned.1.call-update) | async-done | bytes 16400 | tf_op jit(solution)/shard_map/reduce_scatter | solution.py:76
  231.0 46.3 %psum.7 = f32[128,32]{0,1:T(8,128)S(1)} all-reduce(f32[128,32]{0,1:T(8,128)} %reduce-scatter.4.cloned.1.call-done), channel_id=1, replica_groups=mesh['dp'=16,'mem'=16] {'mem'}, use_global_device_ids=true, to_apply=%region_4.5 | all-reduce | flops 4096 | bytes 32768 | tf_op jit(solution)/shard_map/psum | solution.py:76
  278.1 1.5 fusion.27
  279.9 2.3 fusion.28
  284.3 1.4 fusion.29
  285.9 1.2 fusion.65
  288.5 90.3 %all-reduce.3.cloned.1.call-done = f32[2,64,512]{2,1,0:T(8,128)} async-done(((f32[2,64,512]{2,1,0:T(8,128)}), f32[2,64,512]{2,1,0:T(8,128)}) %all-reduce.3.cloned.1.call-update) | async-done | bytes 262160
  379.6 18.1 %all_gather.15 = f32[2,64,512]{2,0,1:T(2,128)S(1)} all-gather(f32[2,4,512]{2,0,1:T(2,128)S(1)} %copy.51), channel_id=1, replica_groups=mesh['dp'=16,'mem'=16] {'mem'}, dimensions={1}, use_global_device_ids=true | all-gather | bytes 278528 | tf_op jit(solution)/shard_map/all_gather | solution.py:118
  398.5 62.8 %reduce-scatter.6.cloned.1.call-done = f32[64,256]{1,0:T(8,128)} async-done(((f32[1024,256]{1,0:T(8,128)}), f32[64,256]{1,0:T(8,128)}) %reduce-scatter.6.cloned.1.call-update) | async-done | bytes 65552 | tf_op jit(solution)/shard_map/reduce_scatter | solution.py:110
  (82 shorter events, 16.4 us)
Async XLA Ops:
  7.2 277.1 %copy-start = (bf16[2,1024,512]{2,1,0:T(8,128)(2,1)S(1)}, bf16[2,1024,512]{2,1,0:T(8,128)(2,1)}, u32[]{:S(2)}) copy-start(bf16[2,1024,512]{2,1,0:T(8,128)(2,1)} %param.16) | copy-start | bytes 6291460
  7.2 53.4 %all-gather.2.cloned.1.call-start = ((), (), s32[]{:S(2)}) async-start(), calls=%async_computation.2 | async-start | bytes 1114112 | tf_op jit(solution)/shard_map/all_gather | solution.py:57
  7.9 223.1 %reduce-scatter.4.cloned.1.call-start = ((), (), s32[]{:S(2)}) async-start(), calls=%async_computation.3 | async-start | bytes 278528 | tf_op jit(solution)/shard_map/reduce_scatter | solution.py:76
  60.5 92.5 %copy-start.6 = (s32[2,128,32]{1,2,0:T(8,128)S(1)}, s32[2,128,32]{1,2,0:T(8,128)}, u32[]{:S(2)}) copy-start(s32[2,128,32]{1,2,0:T(8,128)} %param.14) | copy-start | bytes 98308
  60.8 6.0 %copy-start.2 = (s32[512,32]{1,0:T(8,128)}, s32[512,32]{1,0:T(8,128)S(1)}, u32[]{:S(2)}) copy-start(s32[512,32]{1,0:T(8,128)S(1)} %get-tuple-element.213) | copy-start | bytes 196612 | tf_op jit(solution)/shard_map/while
  61.0 5.8 %copy-start.3 = (s32[512,32]{1,0:T(8,128)}, s32[512,32]{1,0:T(8,128)S(1)}, u32[]{:S(2)}) copy-start(s32[512,32]{1,0:T(8,128)S(1)} %multiply_subtract_fusion.4) | copy-start | bytes 196612 | tf_op jit(solution)/shard_map/while
  83.3 6.0 %copy-start.2 = (s32[512,32]{1,0:T(8,128)}, s32[512,32]{1,0:T(8,128)S(1)}, u32[]{:S(2)}) copy-start(s32[512,32]{1,0:T(8,128)S(1)} %get-tuple-element.213) | copy-start | bytes 196612 | tf_op jit(solution)/shard_map/while
  83.5 5.8 %copy-start.3 = (s32[512,32]{1,0:T(8,128)}, s32[512,32]{1,0:T(8,128)S(1)}, u32[]{:S(2)}) copy-start(s32[512,32]{1,0:T(8,128)S(1)} %multiply_subtract_fusion.4) | copy-start | bytes 196612 | tf_op jit(solution)/shard_map/while
  105.8 6.0 %copy-start.2 = (s32[512,32]{1,0:T(8,128)}, s32[512,32]{1,0:T(8,128)S(1)}, u32[]{:S(2)}) copy-start(s32[512,32]{1,0:T(8,128)S(1)} %get-tuple-element.213) | copy-start | bytes 196612 | tf_op jit(solution)/shard_map/while
  106.0 5.8 %copy-start.3 = (s32[512,32]{1,0:T(8,128)}, s32[512,32]{1,0:T(8,128)S(1)}, u32[]{:S(2)}) copy-start(s32[512,32]{1,0:T(8,128)S(1)} %multiply_subtract_fusion.4) | copy-start | bytes 196612 | tf_op jit(solution)/shard_map/while
  128.3 6.0 %copy-start.2 = (s32[512,32]{1,0:T(8,128)}, s32[512,32]{1,0:T(8,128)S(1)}, u32[]{:S(2)}) copy-start(s32[512,32]{1,0:T(8,128)S(1)} %get-tuple-element.213) | copy-start | bytes 196612 | tf_op jit(solution)/shard_map/while
  128.5 5.8 %copy-start.3 = (s32[512,32]{1,0:T(8,128)}, s32[512,32]{1,0:T(8,128)S(1)}, u32[]{:S(2)}) copy-start(s32[512,32]{1,0:T(8,128)S(1)} %multiply_subtract_fusion.4) | copy-start | bytes 196612 | tf_op jit(solution)/shard_map/while
  150.6 129.2 %copy-start.1 = (f32[256,256]{1,0:T(8,128)}, f32[256,256]{1,0:T(8,128)S(1)}, u32[]{:S(2)}) copy-start(f32[256,256]{1,0:T(8,128)S(1)} %get-tuple-element.135) | copy-start | bytes 786436
  150.6 126.7 %copy-start.5 = (f32[128,32]{0,1:T(8,128)S(1)}, f32[128,32]{0,1:T(8,128)}, u32[]{:S(2)}) copy-start(f32[128,32]{0,1:T(8,128)} %param.13) | copy-start | bytes 49156
  153.0 225.8 %all-reduce.3.cloned.1.call-start = ((), (), s32[]{:S(2)}) async-start(), calls=%async_computation.5 | async-start | bytes 524288
  277.5 0.6 copy-start.7
  279.6 3.7 copy-start.4
  283.3 2.6 copy-start.8
  284.2 177.0 %reduce-scatter.6.cloned.1.call-start = ((), (), s32[]{:S(2)}) async-start(), calls=%async_computation.4 | async-start | bytes 1114112 | tf_op jit(solution)/shard_map/reduce_scatter | solution.py:110
  285.7 1.5 copy-start.9
Sparse Core Ops, SparseCore 0:
  10.4 50.0 all-gather.1
  153.1 77.8 reduce-scatter.3
  284.3 94.4 all-reduce.2
  382.7 78.4 reduce-scatter.5
where the time goes:
time: 469 us; the launch traced here: 468 us
  waiting for transfers between devices  233 us (50%)
  blocking collectives  112 us (24%)
  matrix products  88.4 us (19%)
  local copies, waits for them, and re-layouts  16.8 us (4%)
  between operations  14.6 us (3%)
    unnamed x5, waiting for transfers between devices  91.1 us
    reduce_scatter x1, waiting for transfers between devices, body(): lax.psum_scatter(slot_all, 'dp', scatter_dimension=0, tiled=True)  77.3 us
    reduce_scatter x1, waiting for transfers between devices, body(): lax.psum_scatter(lax.dot_general(dquery, layer_input, (((0,), (0,)), ((),...  62.8 us
    dot_general x4, matrix products, value_block(): jnp.einsum('tbc,tkb->tkc', scores, block_hot.astype(jnp.float32), precisi...  51.8 us
    psum x1, blocking collectives, body(): lax.psum(lax.psum_scatter(slot_all, 'dp', scatter_dimension=0, tiled=True...  46.3 us
    all_gather x1, blocking collectives, body(): row_ids = lax.all_gather(slot_rows, 'dp', axis=0, tiled=True)  25.9 us
    all_gather x1, blocking collectives, body(): row_weights = lax.all_gather(vweights, 'dp', axis=0, tiled=True)  22 us
    dot_general x4, matrix products, value_block(): jnp.einsum('tkb,tkc->tbc', weighted, within_hot, preferred_element_type=j...  19 us
  transfers between devices with their start and end apart: 4, of which 4 were waited for; matrix products, arithmetic and copies ran while one was open for 2% of the time, Pallas kernels for 0%

commit v1 on v0

--- a/solution.py
+++ b/solution.py
@@ -73,7 +73,10 @@
     value_acc, slot_terms = lax.scan(one_block, value_acc, stacked)
     slot_all = slot_terms.reshape(row_count, slot_count)
     value_grad, slot_all = (value_acc, slot_all)
-    slot_grad = lax.psum(lax.psum_scatter(slot_all, "dp", scatter_dimension=0, tiled=True), "mem")
+    slot_grad = jnp.sum(
+        lax.all_gather(lax.psum_scatter(slot_all, "dp", scatter_dimension=0, tiled=True), "mem"),
+        axis=0,
+    )
     centered = slot_grad - jnp.sum(weights * slot_grad, axis=1, keepdims=True)
     score_grad = weights * centered
     own_count = score_grad.shape[0]

time: 469 us -> 439 us (0.936)
  blocking collectives: 112 us -> 86.6 us
  waiting for transfers between devices: 233 us -> 226 us
    psum x1 -> x0, blocking collectives: 46.3 us -> none  [body(): lax.psum(lax.psum_scatter(slot_all, 'dp', scatter_dimension=0, tiled=True...]
    all_gather x0 -> x1, blocking collectives: none -> 20.6 us  [body(): lax.all_gather(lax.psum_scatter(slot_all, 'dp', scatter_dimension=0, tile...]
  transfers between devices with their start and end apart: 4 -> 4, of which waited for: 4 -> 4; matrix products, arithmetic and copies ran while one was open for 2% -> 3% of each run, Pallas kernels for 0% -> 0%
where the time goes in v1:
time: 439 us; the launch traced here: 438 us
  waiting for transfers between devices  226 us (51%)
  matrix products  89.3 us (20%)
  blocking collectives  86.6 us (20%)
  local copies, waits for them, and re-layouts  17.6 us (4%)
  between operations  14.7 us (3%)
    unnamed x5, waiting for transfers between devices  88.4 us
    reduce_scatter x1, waiting for transfers between devices, body(): lax.psum_scatter(slot_all, 'dp', scatter_dimension=0, tiled=True)  72.7 us
    reduce_scatter x1, waiting for transfers between devices, body(): lax.psum_scatter(lax.dot_general(dquery, layer_input, (((0,), (0,)), ((),...  62.8 us
    dot_general x4, matrix products, value_block(): jnp.einsum('tbc,tkb->tkc', scores, block_hot.astype(jnp.float32), precisi...  51.8 us
    all_gather x1, blocking collectives, body(): row_ids = lax.all_gather(slot_rows, 'dp', axis=0, tiled=True)  25.9 us
    all_gather x1, blocking collectives, body(): row_weights = lax.all_gather(vweights, 'dp', axis=0, tiled=True)  22 us
    all_gather x1, blocking collectives, body(): lax.all_gather(lax.psum_scatter(slot_all, 'dp', scatter_dimension=0, tile...  20.6 us
    dot_general x4, matrix products, value_block(): jnp.einsum('tkb,tkc->tbc', weighted, within_hot, preferred_element_type=j...  19 us
  transfers between devices with their start and end apart: 4, of which 4 were waited for; matrix products, arithmetic and copies ran while one was open for 3% of the time, Pallas kernels for 0%

profile of v1, /device:TPU:2, one launch (start us, length us, event | category | flops | bytes accessed | tf_op | source)
XLA Modules:
  0.0 438.3 jit_solution(14544853880277708601)
XLA Ops:
  8.0 25.9 %all_gather.18 = s32[2048,32]{0,1:T(8,128)} all-gather(s32[128,32]{0,1:T(8,128)} %param.12), channel_id=1, replica_groups=mesh['dp'=16,'mem'=16] {'dp'}, dimensions={0}, use_global_device_ids=true | all-gather | bytes 278528 | tf_op jit(solution)/shard_map/all_gather | solution.py:58
  33.8 1.3 copy.53
  35.9 22.0 %all_gather.19 = bf16[2048,32]{0,1:T(8,128)(2,1)S(1)} all-gather(bf16[128,32]{0,1:T(8,128)(2,1)S(1)} %convert_element_type.41), channel_id=1, replica_groups=mesh['dp'=16,'mem'=16] {'dp'}, dimensions={0}, use_global_device_ids=true | all-gather | bytes 139264 | tf_op jit(solution)/shard_map/all_gather | solution.py:59
  58.8 1.7 all-gather.3.cloned.1.call-done
  60.5 90.0 %while.15 = (s32[]{:T(128)}, f32[256,256]{1,0:T(8,128)S(1)}, f32[4,512,32]{2,1,0:T(8,128)}, s32[4,512,32]{2,1,0:T(8,128)S(1)}, s32[]{:T(128)}, /*index=5*/bf16[4...) while((s32[]{:T(128)}, f32[256,256]{1,0:T(8,128)S(1)}, ...), condition=%wide.region_2.3_spmd.clone, body=%wide.region_0.2_spmd.clone.sunk | while | flops 206569472 | bytes 4358351 | solution.py:73
  61.0 1.0 dynamic-slice_bitcast_fusion.2
  62.0 4.8 %fusion.85 = bf16[512,2,128]{2,1,0:T(2,128)(2,1)} fusion(s32[512,32]{1,0:T(8,128)S(1)} %multiply_subtract_fusion.4, pred[512,32]{1,0:T(8,128)(4,1)S(1)} %get-tuple-element.215, s32[512,32]{1,0:T(8,128)S(1)} %get-tuple-element.216, bf16[512,32]{1,0:T(8,128)(2,1)S(1)} %dynamic-slice_bitcast_fusion.2), kind=kOutput, calls=%fused_computation.5.clone.1 | convolution fusion | flops 10715136 | bytes 442368 | tf_op jit(solution)/shard_map/while/body/eval_jaxpr/tkb,tkc->tbc/dot_general | solution.py:29
  66.8 1.3 convolution_add_fusion.2
  68.1 1.2 fusion.86
  69.4 13.0 %multiply_reduce_fusion.3 = f32[512,32]{1,0:T(8,128)S(1)} fusion(s32[512,32]{1,0:T(8,128)} %copy-done.3, f32[512,2,128]{2,0,1:T(8,128)S(1)} %fusion.86, pred[512,32]{1,0:T(8,128)(4,1)S(1)} %get-tuple-element.215, s32[512,32]{1,0:T(8,128)} %copy-done.2), kind=kOutput, calls=%fused_computation.clone.1 | convolution fusion | flops 60866560 | bytes 737280 | tf_op jit(solution)/shard_map/while/body/eval_jaxpr/tbc,tkb->tkc/dot_general | solution.py:38
  83.5 1.0 dynamic-slice_bitcast_fusion.2
  84.5 4.8 %fusion.85 = bf16[512,2,128]{2,1,0:T(2,128)(2,1)} fusion(s32[512,32]{1,0:T(8,128)S(1)} %multiply_subtract_fusion.4, pred[512,32]{1,0:T(8,128)(4,1)S(1)} %get-tuple-element.215, s32[512,32]{1,0:T(8,128)S(1)} %get-tuple-element.216, bf16[512,32]{1,0:T(8,128)(2,1)S(1)} %dynamic-slice_bitcast_fusion.2), kind=kOutput, calls=%fused_computation.5.clone.1 | convolution fusion | flops 10715136 | bytes 442368 | tf_op jit(solution)/shard_map/while/body/eval_jaxpr/tkb,tkc->tbc/dot_general | solution.py:29
  89.3 1.3 convolution_add_fusion.2
  90.6 1.2 fusion.86
  91.9 13.0 %multiply_reduce_fusion.3 = f32[512,32]{1,0:T(8,128)S(1)} fusion(s32[512,32]{1,0:T(8,128)} %copy-done.3, f32[512,2,128]{2,0,1:T(8,128)S(1)} %fusion.86, pred[512,32]{1,0:T(8,128)(4,1)S(1)} %get-tuple-element.215, s32[512,32]{1,0:T(8,128)} %copy-done.2), kind=kOutput, calls=%fused_computation.clone.1 | convolution fusion | flops 60866560 | bytes 737280 | tf_op jit(solution)/shard_map/while/body/eval_jaxpr/tbc,tkb->tkc/dot_general | solution.py:38
  107.0 4.8 %fusion.85 = bf16[512,2,128]{2,1,0:T(2,128)(2,1)} fusion(s32[512,32]{1,0:T(8,128)S(1)} %multiply_subtract_fusion.4, pred[512,32]{1,0:T(8,128)(4,1)S(1)} %get-tuple-element.215, s32[512,32]{1,0:T(8,128)S(1)} %get-tuple-element.216, bf16[512,32]{1,0:T(8,128)(2,1)S(1)} %dynamic-slice_bitcast_fusion.2), kind=kOutput, calls=%fused_computation.5.clone.1 | convolution fusion | flops 10715136 | bytes 442368 | tf_op jit(solution)/shard_map/while/body/eval_jaxpr/tkb,tkc->tbc/dot_general | solution.py:29
  111.8 1.3 convolution_add_fusion.2
  113.1 1.2 fusion.86
  114.4 13.0 %multiply_reduce_fusion.3 = f32[512,32]{1,0:T(8,128)S(1)} fusion(s32[512,32]{1,0:T(8,128)} %copy-done.3, f32[512,2,128]{2,0,1:T(8,128)S(1)} %fusion.86, pred[512,32]{1,0:T(8,128)(4,1)S(1)} %get-tuple-element.215, s32[512,32]{1,0:T(8,128)} %copy-done.2), kind=kOutput, calls=%fused_computation.clone.1 | convolution fusion | flops 60866560 | bytes 737280 | tf_op jit(solution)/shard_map/while/body/eval_jaxpr/tbc,tkb->tkc/dot_general | solution.py:38
  129.5 4.8 %fusion.85 = bf16[512,2,128]{2,1,0:T(2,128)(2,1)} fusion(s32[512,32]{1,0:T(8,128)S(1)} %multiply_subtract_fusion.4, pred[512,32]{1,0:T(8,128)(4,1)S(1)} %get-tuple-element.215, s32[512,32]{1,0:T(8,128)S(1)} %get-tuple-element.216, bf16[512,32]{1,0:T(8,128)(2,1)S(1)} %dynamic-slice_bitcast_fusion.2), kind=kOutput, calls=%fused_computation.5.clone.1 | convolution fusion | flops 10715136 | bytes 442368 | tf_op jit(solution)/shard_map/while/body/eval_jaxpr/tkb,tkc->tbc/dot_general | solution.py:29
  134.3 1.3 convolution_add_fusion.2
  135.6 1.2 fusion.86
  136.9 13.0 %multiply_reduce_fusion.3 = f32[512,32]{1,0:T(8,128)S(1)} fusion(s32[512,32]{1,0:T(8,128)} %copy-done.3, f32[512,2,128]{2,0,1:T(8,128)S(1)} %fusion.86, pred[512,32]{1,0:T(8,128)(4,1)S(1)} %get-tuple-element.215, s32[512,32]{1,0:T(8,128)} %copy-done.2), kind=kOutput, calls=%fused_computation.clone.1 | convolution fusion | flops 60866560 | bytes 737280 | tf_op jit(solution)/shard_map/while/body/eval_jaxpr/tbc,tkb->tkc/dot_general | solution.py:38
  156.6 72.7 %reduce-scatter.4.cloned.1.call-done = f32[128,32]{1,0:T(8,128)} async-done(((f32[2048,32]{1,0:T(8,128)}), f32[128,32]{1,0:T(8,128)}) %reduce-scatter.4.cloned.1.call-update) | async-done | bytes 16400 | tf_op jit(solution)/shard_map/reduce_scatter | solution.py:77
  229.3 20.6 %all-gather = f32[2048,32]{1,0:T(8,128)S(1)} all-gather(f32[128,32]{1,0:T(8,128)} %reduce-scatter.4.cloned.1.call-done), channel_id=2, replica_groups=mesh['dp'=16,'mem'=16] {'mem'}, dimensions={0}, use_global_device_ids=true | all-gather | bytes 278528 | tf_op jit(solution)/shard_map/all_gather | solution.py:77
  250.3 2.3 fusion.27
  253.1 2.3 fusion.28
  257.4 1.4 fusion.29
  259.0 1.3 fusion.65
  261.6 87.7 %all-reduce.3.cloned.1.call-done = f32[2,64,512]{2,1,0:T(8,128)} async-done(((f32[2,64,512]{2,1,0:T(8,128)}), f32[2,64,512]{2,1,0:T(8,128)}) %all-reduce.3.cloned.1.call-update) | async-done | bytes 262160
  350.1 18.1 %all_gather.23 = f32[2,64,512]{2,0,1:T(2,128)S(1)} all-gather(f32[2,4,512]{2,0,1:T(2,128)S(1)} %copy.67), channel_id=1, replica_groups=mesh['dp'=16,'mem'=16] {'mem'}, dimensions={1}, use_global_device_ids=true | all-gather | bytes 278528 | tf_op jit(solution)/shard_map/all_gather | solution.py:121
  369.0 62.8 %reduce-scatter.6.cloned.1.call-done = f32[64,256]{1,0:T(8,128)} async-done(((f32[1024,256]{1,0:T(8,128)}), f32[64,256]{1,0:T(8,128)}) %reduce-scatter.6.cloned.1.call-update) | async-done | bytes 65552 | tf_op jit(solution)/shard_map/reduce_scatter | solution.py:113
  (90 shorter events, 20.2 us)
Async XLA Ops:
  7.2 250.2 %copy-start = (bf16[2,1024,512]{2,1,0:T(8,128)(2,1)S(1)}, bf16[2,1024,512]{2,1,0:T(8,128)(2,1)}, u32[]{:S(2)}) copy-start(bf16[2,1024,512]{2,1,0:T(8,128)(2,1)} %param.16) | copy-start | bytes 6291460
  7.2 53.4 %all-gather.3.cloned.1.call-start = ((), (), s32[]{:S(2)}) async-start(), calls=%async_computation.2 | async-start | bytes 1114112 | tf_op jit(solution)/shard_map/all_gather | solution.py:57
  7.9 221.4 %reduce-scatter.4.cloned.1.call-start = ((), (), s32[]{:S(2)}) async-start(), calls=%async_computation.3 | async-start | bytes 1114112 | tf_op jit(solution)/shard_map/reduce_scatter | solution.py:77
  60.5 90.1 %copy-start.6 = (s32[2,128,32]{1,2,0:T(8,128)S(1)}, s32[2,128,32]{1,2,0:T(8,128)}, u32[]{:S(2)}) copy-start(s32[2,128,32]{1,2,0:T(8,128)} %param.14) | copy-start | bytes 98308
  60.5 90.2 %copy-start.5 = (f32[128,32]{0,1:T(8,128)S(1)}, f32[128,32]{0,1:T(8,128)}, u32[]{:S(2)}) copy-start(f32[128,32]{0,1:T(8,128)} %param.13) | copy-start | bytes 49156
  60.8 6.0 %copy-start.2 = (s32[512,32]{1,0:T(8,128)}, s32[512,32]{1,0:T(8,128)S(1)}, u32[]{:S(2)}) copy-start(s32[512,32]{1,0:T(8,128)S(1)} %get-tuple-element.216) | copy-start | bytes 196612 | tf_op jit(solution)/shard_map/while
  61.0 5.8 %copy-start.3 = (s32[512,32]{1,0:T(8,128)}, s32[512,32]{1,0:T(8,128)S(1)}, u32[]{:S(2)}) copy-start(s32[512,32]{1,0:T(8,128)S(1)} %multiply_subtract_fusion.4) | copy-start | bytes 196612 | tf_op jit(solution)/shard_map/while
  83.3 6.0 %copy-start.2 = (s32[512,32]{1,0:T(8,128)}, s32[512,32]{1,0:T(8,128)S(1)}, u32[]{:S(2)}) copy-start(s32[512,32]{1,0:T(8,128)S(1)} %get-tuple-element.216) | copy-start | bytes 196612 | tf_op jit(solution)/shard_map/while
  83.5 5.8 %copy-start.3 = (s32[512,32]{1,0:T(8,128)}, s32[512,32]{1,0:T(8,128)S(1)}, u32[]{:S(2)}) copy-start(s32[512,32]{1,0:T(8,128)S(1)} %multiply_subtract_fusion.4) | copy-start | bytes 196612 | tf_op jit(solution)/shard_map/while
  105.8 6.0 %copy-start.2 = (s32[512,32]{1,0:T(8,128)}, s32[512,32]{1,0:T(8,128)S(1)}, u32[]{:S(2)}) copy-start(s32[512,32]{1,0:T(8,128)S(1)} %get-tuple-element.216) | copy-start | bytes 196612 | tf_op jit(solution)/shard_map/while
  106.0 5.8 %copy-start.3 = (s32[512,32]{1,0:T(8,128)}, s32[512,32]{1,0:T(8,128)S(1)}, u32[]{:S(2)}) copy-start(s32[512,32]{1,0:T(8,128)S(1)} %multiply_subtract_fusion.4) | copy-start | bytes 196612 | tf_op jit(solution)/shard_map/while
  128.3 6.0 %copy-start.2 = (s32[512,32]{1,0:T(8,128)}, s32[512,32]{1,0:T(8,128)S(1)}, u32[]{:S(2)}) copy-start(s32[512,32]{1,0:T(8,128)S(1)} %get-tuple-element.216) | copy-start | bytes 196612 | tf_op jit(solution)/shard_map/while
  128.5 5.8 %copy-start.3 = (s32[512,32]{1,0:T(8,128)}, s32[512,32]{1,0:T(8,128)S(1)}, u32[]{:S(2)}) copy-start(s32[512,32]{1,0:T(8,128)S(1)} %multiply_subtract_fusion.4) | copy-start | bytes 196612 | tf_op jit(solution)/shard_map/while
  150.6 99.7 %copy-start.1 = (f32[256,256]{1,0:T(8,128)}, f32[256,256]{1,0:T(8,128)S(1)}, u32[]{:S(2)}) copy-start(f32[256,256]{1,0:T(8,128)S(1)} %get-tuple-element.138) | copy-start | bytes 786436
  150.6 198.7 %all-reduce.3.cloned.1.call-start = ((), (), s32[]{:S(2)}) async-start(), calls=%async_computation.5 | async-start | bytes 524288
  250.2 2.9 copy-start.7
  250.2 2.9 copy-start.8
  250.2 2.9 copy-start.11
  250.3 2.6 copy-start.9
  252.7 3.8 copy-start.4
  256.4 2.6 copy-start.10
  257.4 174.4 %reduce-scatter.6.cloned.1.call-start = ((), (), s32[]{:S(2)}) async-start(), calls=%async_computation.4 | async-start | bytes 1114112 | tf_op jit(solution)/shard_map/reduce_scatter | solution.py:113
  258.8 1.5 copy-start.12
Sparse Core Ops, SparseCore 0:
  10.4 50.0 all-gather.2
  150.7 78.5 reduce-scatter.3
  257.5 91.7 all-reduce.2
  353.2 78.4 reduce-scatter.5
